TPU v7x, 32 devices: a whole 2x2x4 slice. The times are simulated.
32 devices in a mesh: ia: 8 (over y, x, core), ja: 4 (over z).
Axes of the slice: x: 2, y: 2, z: 4, core: 2. Of those that a mesh axis runs over, the one named last changes fastest.
Arguments:
- slabs: bfloat16 [32, 512, 512], P(('ia', 'ja')), may hold values from -1.1953125 to 1.1953125
- pno_coef: bfloat16 [512, 256, 128], P(('ia', 'ja')), may hold values from -0.375 to 0.375
- dom_blocks: int32 [512, 2], P(('ia', 'ja')), may hold values from 0 to 3, as said below
- pair_first: int32 [512], P(('ia', 'ja')), may hold values from 0 to 3
- pair_second: int32 [512], P(('ia', 'ja')), may hold values from 0 to 7
- pno_energy: float32 [512, 128], P(('ia', 'ja')), may hold values from 0.3 to 3
- pair_shift: float32 [512], P(('ia', 'ja')), may hold values from 0.5 to 2
- margin_i: bfloat16 [512, 16, 128, 128], P(('ia', 'ja')), may hold values from -0.5 to 0.5
- margin_j: bfloat16 [512, 16, 128, 128], P(('ia', 'ja')), may hold values from -0.5 to 0.5
- couple_i: float32 [512, 16], P(('ia', 'ja')), may hold values from -0.45 to 0.45
- couple_j: float32 [512, 16], P(('ia', 'ja')), may hold values from -0.45 to 0.45
- ask_i: int32 [32, 8, 4], P(('ia', 'ja')), may hold values from 0 to 15, as said below
- ask_j: int32 [32, 4, 4], P(('ia', 'ja')), may hold values from 0 to 15, as said below
- link_i: int32 [512, 16], P(('ia', 'ja')), may hold values from 0 to 31, as said below
- link_j: int32 [512, 16], P(('ia', 'ja')), may hold values from 0 to 15, as said below
Outputs:
- amplitudes: float32 [512, 128, 128], P(('ia', 'ja'))
- density: float32 [512, 512], P(('ia', 'ja'))
Inputs may be any that keep to these rules, and one draw needn't show every extreme that they name: `dom_blocks`: the 2 blocks of a pair are distinct. `ask_i`: for each block g and each peer s, the 4 slots are distinct. `ask_j`: for each block g and each peer s, the 4 slots are distinct. `link_i`: within each aligned block of 16 pairs every value is named at least once. `link_j`: within each aligned block of 16 pairs every value is named at least once.
All inputs are finite; a program needn't handle non-finite values.
Results may differ from a plain program's by a relative error of at most 0.0045.
Values may be sent and summed in bfloat16 or wider, within the bound.
A program may use at most 128 MiB of HBM per device.

v0:
```python
import functools
import math

import jax
import jax.numpy as jnp
from jax import lax
from jax.experimental import pallas as pl
from jax.experimental.pallas import tpu as pltpu
from jax.sharding import PartitionSpec as P

BLK = 128
ITERS = 2
MESH = pl.DeviceIdType.MESH
F32 = jnp.float32
BF16 = jnp.bfloat16


def matmul(a, b, da, db):
    return lax.dot_general(a, b, (((da,), (db,)), ((), ())), preferred_element_type=F32)


def enter(n_ia, n_ja, ia, ja):
    barrier = pltpu.get_barrier_semaphore()
    for k in range(1, n_ia):
        pl.semaphore_signal(
            barrier, inc=1, device_id=(lax.rem(ia + k, n_ia), ja), device_id_type=MESH
        )
    for k in range(1, n_ja):
        pl.semaphore_signal(
            barrier, inc=1, device_id=(ia, lax.rem(ja + k, n_ja)), device_id_type=MESH
        )
    pl.semaphore_wait(barrier, n_ia + n_ja - 2)


def remote(src, dst, send, recv, device):
    return pltpu.make_async_remote_copy(
        src_ref=src, dst_ref=dst, send_sem=send, recv_sem=recv, device_id=device,
        device_id_type=MESH,
    )


def exchange_kernel(
    n_ia, n_ja,
    slabs, ask_i, ask_j, coef, dom, first, second,
    exch, all_i, all_j,
    row_slabs, col_slabs,
    loc, row_s, row_r, col_s, col_r, fwd_s, fwd_r, ai_s, ai_r, aj_s, aj_r,
):
    ia, ja = lax.axis_index("ia"), lax.axis_index("ja")
    half = n_ia // 2
    partner = ia + 1 - 2 * lax.rem(ia, 2)
    locals_ = [
        pltpu.make_async_copy(slabs, row_slabs.at[ja], loc.at[0]),
        pltpu.make_async_copy(slabs, col_slabs.at[ia], loc.at[1]),
        pltpu.make_async_copy(ask_i.at[0], all_i.at[ia], loc.at[2]),
        pltpu.make_async_copy(ask_j.at[0], all_j.at[ja], loc.at[3]),
    ]
    for c in locals_:
        c.start()
    enter(n_ia, n_ja, ia, ja)
    rows = [
        remote(slabs, row_slabs.at[ja], row_s.at[k], row_r.at[k], (ia, lax.rem(ja + k, n_ja)))
        for k in range(1, n_ja)
    ]
    cols = [
        remote(slabs, col_slabs.at[ia], col_s.at[k], col_r.at[k],
               (lax.rem(ia + 2 * k, n_ia), ja))
        for k in range(1, half)
    ]
    own = remote(slabs, col_slabs.at[ia], fwd_s.at[0], fwd_r.at[0], (partner, ja))
    asks = [
        remote(ask_i.at[0], all_i.at[ia], ai_s.at[k], ai_r.at[k], (lax.rem(ia + k, n_ia), ja))
        for k in range(1, n_ia)
    ] + [
        remote(ask_j.at[0], all_j.at[ja], aj_s.at[k], aj_r.at[k], (ia, lax.rem(ja + k, n_ja)))
        for k in range(1, n_ja)
    ]
    for c in cols + rows + [own] + asks:
        c.start()
    forwards = [own]
    for k in range(1, half):
        source = lax.rem(ia + n_ia - 2 * k, n_ia)
        cols[k - 1].wait_recv()
        f = remote(col_slabs.at[source], col_slabs.at[source], fwd_s.at[k], fwd_r.at[k],
                   (partner, ja))
        f.start()
        forwards.append(f)
    for c in locals_:
        c.wait()
    for c in rows + forwards:
        c.wait_recv()

    def project(p, carry):
        f, s, d0, d1 = first[p], second[p], dom[p, 0], dom[p, 1]
        both = jnp.concatenate(
            [
                jnp.concatenate([row_slabs[f, d0], row_slabs[f, d1]], axis=0),
                jnp.concatenate([col_slabs[s, d0], col_slabs[s, d1]], axis=0),
            ],
            axis=1,
        )
        projected = matmul(coef[p], both, 0, 0).astype(BF16)
        aux = projected.shape[1] // 2
        exch[p] = matmul(projected[:, :aux], projected[:, aux:], 1, 1)
        return carry

    lax.fori_loop(0, coef.shape[0], project, 0)
    for c in asks:
        c.wait_recv()
    for c in rows + cols + forwards + asks:
        c.wait_send()


def amplitude_kernel(
    n_ia, n_ja, factor,
    exch, energy, shift, coef, margin_i, margin_j, cpl_i, cpl_j, link_i, link_j, all_i, all_j,
    dom,
    amp, dens,
    sent, mi, mj, acc, stage_i, stage_j, tables_i, tables_j, mf, cf, own, out1, in1, out2, in2,
    m_sem, is_, ir_, js_, jr_, s1, r1, s2, r2,
):
    ia, ja = lax.axis_index("ia"), lax.axis_index("ja")
    pairs = exch.shape[0]
    slots_i, slots_j = all_i.shape[2], all_j.shape[2]
    loads = [
        pltpu.make_async_copy(margin_j, mj, m_sem.at[0]),
        pltpu.make_async_copy(margin_i, mi, m_sem.at[1]),
    ]
    for c in loads:
        c.start()

    def denominator(p):
        e = jnp.broadcast_to(energy[pl.ds(p, 1), :], exch.shape[1:])
        return e + e.T + shift[p]

    def begin(p, carry):
        sent[p] = (-exch[p] / denominator(p)).astype(BF16)
        return carry

    lax.fori_loop(0, pairs, begin, 0)
    enter(n_ia, n_ja, ia, ja)

    def couple(p, table, margin, weights, link, total):
        for n in range(0, margin.shape[1], 2):
            sides, margins = [], []
            for m in (n, n + 1):
                block = margin[p, m]
                left = matmul(block, table[link[p, m]], 1, 0)
                sides.append((left * weights[p, m]).astype(BF16))
                margins.append(block)
            part = matmul(
                jnp.concatenate(sides, axis=1), jnp.concatenate(margins, axis=1), 1, 1
            )
            total = part if total is None else total + part
        return total

    for it in range(ITERS):
        copies_i, copies_j = [], []
        table_i, table_j = tables_i[it], tables_j[it]
        for k in range(1, n_ja):
            peer = lax.rem(ja + k, n_ja)
            for slot in range(slots_j):
                stage_j[it, k, slot] = sent[all_j[peer, ja, slot]]
            c = remote(stage_j.at[it, k], table_j.at[pl.ds(ja * slots_j, slots_j)],
                       js_.at[it, k], jr_.at[it, k], (ia, peer))
            c.start()
            copies_j.append(c)
        for k in range(1, n_ia):
            peer = lax.rem(ia + k, n_ia)
            for slot in range(slots_i):
                stage_i[it, k, slot] = sent[all_i[peer, ia, slot]]
            c = remote(stage_i.at[it, k], table_i.at[pl.ds(ia * slots_i, slots_i)],
                       is_.at[it, k], ir_.at[it, k], (peer, ja))
            c.start()
            copies_i.append(c)
        for slot in range(slots_j):
            table_j[ja * slots_j + slot] = sent[all_j[ja, ja, slot]]
        for slot in range(slots_i):
            table_i[ia * slots_i + slot] = sent[all_i[ia, ia, slot]]
        if it == 0:
            loads[0].wait()
        for c in copies_j:
            c.wait_recv()

        def second_kind(p, carry, table_j=table_j):
            acc[p] = couple(p, table_j, mj, cpl_j, link_j, None)
            return carry

        lax.fori_loop(0, pairs, second_kind, 0)
        if it == 0:
            loads[1].wait()
        for c in copies_i:
            c.wait_recv()

        def first_kind(p, carry, it=it, table_i=table_i):
            total = couple(p, table_i, mi, cpl_i, link_i, acc[p])
            new = -(exch[p] + total) / denominator(p)
            if it == ITERS - 1:
                amp[p] = new
            sent[p] = new.astype(BF16)
            return carry

        lax.fori_loop(0, pairs, first_kind, 0)
        for c in copies_i + copies_j:
            c.wait_send()

    blocks = mf.shape[1] // BLK

    def spread(p, carry):
        s = sent[p]
        square = (matmul(s, s, 1, 1) + matmul(s, s, 0, 0)).astype(BF16)
        c = coef[p]
        mapped = matmul(c, square, 1, 0).astype(BF16)
        d0, d1 = dom[p, 0], dom[p, 1]
        for b in range(blocks):
            k0 = jnp.where(d0 == b, 1.0, 0.0).astype(F32)
            k1 = jnp.where(d1 == b, 1.0, 0.0).astype(F32)
            where = pl.ds(b * BLK, BLK)
            mf[p, where] = (
                mapped[:BLK].astype(F32) * k0 + mapped[BLK:].astype(F32) * k1
            ).astype(BF16)
            cf[p, where] = (c[:BLK].astype(F32) * k0 + c[BLK:].astype(F32) * k1).astype(BF16)
        return carry

    lax.fori_loop(0, pairs, spread, 0)
    chunk = own.shape[0]

    def partial_rows(peer):
        start = pl.multiple_of(peer * chunk, chunk)
        total = None
        for p in range(0, pairs, 2):
            a = jnp.concatenate([mf[p, pl.ds(start, chunk)], mf[p + 1, pl.ds(start, chunk)]], 1)
            b = jnp.concatenate([cf[p], cf[p + 1]], 1)
            part = matmul(a, b, 1, 1)
            total = part if total is None else total + part
        return total

    sends = []
    for k in range(1, n_ia):
        peer = lax.rem(ia + k, n_ia)
        out1[k] = partial_rows(peer).astype(BF16)
        c = remote(out1.at[k], in1.at[k], s1.at[k], r1.at[k], (peer, ja))
        c.start()
        sends.append(c)
    own[...] = partial_rows(ia)
    for k in range(1, n_ia):
        sends[k - 1].wait_recv()
        own[...] += in1[k].astype(F32)
    piece = dens.shape[0]
    for j in range(n_ja):
        out2[j] = own[pl.ds(j * piece, piece), :]
    last = []
    for k in range(1, n_ja):
        peer = lax.rem(ja + k, n_ja)
        c = remote(out2.at[peer], in2.at[k], s2.at[k], r2.at[k], (ia, peer))
        c.start()
        last.append(c)
    total = out2[ja]
    for k in range(1, n_ja):
        last[k - 1].wait_recv()
        total = total + in2[k]
    dens[...] = total * factor
    for c in sends + last:
        c.wait_send()


def body(
    slabs, pno_coef, dom_blocks, pair_first, pair_second, pno_energy, pair_shift,
    margin_i, margin_j, couple_i, couple_j, ask_i, ask_j, link_i, link_j,
):
    n_ia, n_ja = lax.axis_size("ia"), lax.axis_size("ja")
    devices = n_ia * n_ja
    pairs, domain, pno = pno_coef.shape
    pao, aux = slabs.shape[1:]
    blocks = pao // BLK
    slots_i, slots_j = ask_i.shape[2], ask_j.shape[2]
    links_i, links_j = margin_i.shape[1], margin_j.shape[1]
    vmem = pl.BlockSpec(memory_space=pltpu.VMEM)
    smem = pl.BlockSpec(memory_space=pltpu.SMEM)
    anym = pl.BlockSpec(memory_space=pl.ANY)
    hbm = pl.BlockSpec(memory_space=pltpu.HBM)
    dma = pltpu.SemaphoreType.DMA
    exch, all_i, all_j = pl.pallas_call(
        functools.partial(exchange_kernel, n_ia, n_ja),
        out_shape=(
            jax.ShapeDtypeStruct((pairs, pno, pno), F32),
            jax.ShapeDtypeStruct((n_ia,) + ask_i.shape[1:], jnp.int32),
            jax.ShapeDtypeStruct((n_ja,) + ask_j.shape[1:], jnp.int32),
        ),
        in_specs=[hbm, hbm, hbm, vmem, smem, smem, smem],
        out_specs=(vmem, hbm, hbm),
        scratch_shapes=[
            pltpu.VMEM((n_ja, blocks, BLK, aux), BF16),
            pltpu.VMEM((n_ia, blocks, BLK, aux), BF16),
            dma((4,)),
            dma((n_ja,)), dma((n_ja,)),
            dma((n_ia,)), dma((n_ia,)),
            dma((n_ia,)), dma((n_ia,)),
            dma((n_ia,)), dma((n_ia,)),
            dma((n_ja,)), dma((n_ja,)),
        ],
        compiler_params=pltpu.CompilerParams(collective_id=0, has_side_effects=True),
        name="exchange",
    )(slabs.reshape(blocks, BLK, aux), ask_i, ask_j, pno_coef, dom_blocks, pair_first,
      pair_second)
    factor = 1.0 / math.sqrt(pairs * devices)
    chunk, piece = pao // n_ia, pao // devices
    return pl.pallas_call(
        functools.partial(amplitude_kernel, n_ia, n_ja, factor),
        out_shape=(
            jax.ShapeDtypeStruct((pairs, pno, pno), F32),
            jax.ShapeDtypeStruct((piece, pao), F32),
        ),
        in_specs=[vmem, vmem, smem, vmem, hbm, hbm, smem, smem, smem, smem, smem, smem, smem],
        out_specs=(vmem, vmem),
        scratch_shapes=[
            pltpu.VMEM((pairs, pno, pno), BF16),
            pltpu.VMEM((pairs, links_i, pno, pno), BF16),
            pltpu.VMEM((pairs, links_j, pno, pno), BF16),
            pltpu.VMEM((pairs, pno, pno), F32),
            pltpu.VMEM((ITERS, n_ia, slots_i, pno, pno), BF16),
            pltpu.VMEM((ITERS, n_ja, slots_j, pno, pno), BF16),
            [pltpu.VMEM((n_ia * slots_i, pno, pno), BF16)] * ITERS,
            [pltpu.VMEM((n_ja * slots_j, pno, pno), BF16)] * ITERS,
            pltpu.VMEM((pairs, pao, pno), BF16),
            pltpu.VMEM((pairs, pao, pno), BF16),
            pltpu.VMEM((chunk, pao), F32),
            pltpu.VMEM((n_ia, chunk, pao), BF16),
            pltpu.VMEM((n_ia, chunk, pao), BF16),
            pltpu.VMEM((n_ja, piece, pao), F32),
            pltpu.VMEM((n_ja, piece, pao), F32),
            dma((2,)),
            dma((ITERS, n_ia)), dma((ITERS, n_ia)),
            dma((ITERS, n_ja)), dma((ITERS, n_ja)),
            dma((n_ia,)), dma((n_ia,)),
            dma((n_ja,)), dma((n_ja,)),
        ],
        compiler_params=pltpu.CompilerParams(collective_id=1, has_side_effects=True),
        name="amplitudes",
    )(exch, pno_energy, pair_shift, pno_coef, margin_i, margin_j, couple_i, couple_j,
      link_i, link_j, all_i, all_j, dom_blocks)


def solution(mesh):
    both = ("ia", "ja")
    in_specs = (
        P(both, None, None), P(both, None, None), P(both, None), P(both), P(both),
        P(both, None), P(both), P(both, None, None, None), P(both, None, None, None),
        P(both, None), P(both, None), P(both, None, None), P(both, None, None),
        P(both, None), P(both, None),
    )
    out_specs = (P(both, None, None), P(both, None))
    return jax.shard_map(body, mesh=mesh, in_specs=in_specs, out_specs=out_specs, check_vma=False)
```

profile of v0, /device:TPU:0, one launch (start us, length us, event | category | flops | bytes accessed | tf_op | source)
XLA Modules:
  0.0 157.5 jit_solution(6372472290000754544)
XLA Ops:
  0.6 1.3 copy.17.ask_i
  2.0 1.4 copy.18.dom
  3.3 56.0 %exchange.1 = (f32[16,128,128]{2,1,0:T(8,128)}, s32[8,8,4]{2,1,0:T(8,128)}, s32[4,4,4]{2,1,0:T(4,128)}) custom-call(bf16[4,128,512]{2,1,0:T(8,128)(2,1)} %bitcast.1, s32[1,8,4]{2,1,0:T(8,128)} %copy.17.ask_i, s32[1,4,4]{2,1,0:T(4,128)} %ask_j.1, bf16[16,256,128]{2,1,0:T(8,128)(2,1)} %coef.3, s32[16,2]{1,0:T(8,128)} %copy.18.dom, s32[16]{0:T(128)} %first.1, ...), custom_call_target="tpu_custom_call" | custom-call | tf_op jit(solution)/shard_map/exchange/pallas_call | solution.py:283
  59.3 94.5 %amplitudes.1 = (f32[16,128,128]{2,1,0:T(8,128)}, f32[16,512]{1,0:T(8,128)}) custom-call(f32[16,128,128]{2,1,0:T(8,128)} %get-tuple-element.5.exch, f32[16,128]{1,0:T(8,128)} %energy.1, f32[16]{0:T(128)} %shift.1, bf16[16,256,128]{2,1,0:T(8,128)(2,1)} %coef.3, bf16[16,16,128,128]{3,2,1,0:T(8,128)(2,1)} %margin_i.1, bf16[16,16,128,128]{3,2,1,0:T(8,128)(2,1)} %margin_j.1, ...), custom_call_target="tpu_custom_call" | custom-call | tf_op jit(solution)/shard_map/amplitudes/pallas_call | solution.py:308
  153.9 2.3 %copy.22 = f32[16,128,128]{2,1,0:T(8,128)} copy(f32[16,128,128]{2,1,0:T(8,128)} %get-tuple-element.10) | data formatting | bytes 2097152
  156.2 1.4 copy.23
where the time goes:
time: 158 us
  Pallas kernels  151 us (96%)
  local copies, waits for them, and re-layouts  6.37 us (4%)
    pallas_call x1, Pallas kernels, body(): pl.pallas_call(functools.partial(amplitude_kernel, n_ia, n_ja, factor), o...  94.5 us
    pallas_call x1, Pallas kernels, body(): pl.pallas_call(functools.partial(exchange_kernel, n_ia, n_ja), out_shape=...  56 us
    unnamed x4, local copies, waits for them, and re-layouts  6.37 us

commit v1 on v0

--- a/solution.py
+++ b/solution.py
@@ -43,8 +43,8 @@
     n_ia, n_ja,
     slabs, ask_i, ask_j, coef, dom, first, second,
     exch, all_i, all_j,
-    row_slabs, col_slabs,
-    loc, row_s, row_r, col_s, col_r, fwd_s, fwd_r, ai_s, ai_r, aj_s, aj_r,
+    row_slabs, col_slabs, proj,
+    loc, up_s, up_r, dn_s, dn_r, col_s, col_r, fwd_s, fwd_r, ai_s, ai_r, aj_s, aj_r,
 ):
     ia, ja = lax.axis_index("ia"), lax.axis_index("ja")
     half = n_ia // 2
@@ -58,10 +58,40 @@
     for c in locals_:
         c.start()
     enter(n_ia, n_ja, ia, ja)
-    rows = [
-        remote(slabs, row_slabs.at[ja], row_s.at[k], row_r.at[k], (ia, lax.rem(ja + k, n_ja)))
-        for k in range(1, n_ja)
-    ]
+    blocks = slabs.shape[0]
+
+    def up(t, c):
+        at = ja - t
+        src = slabs.at[c] if t == 0 else row_slabs.at[at, c]
+        return remote(src, row_slabs.at[at, c], up_s.at[t, c], up_r.at[t, c], (ia, ja + 1))
+
+    def down(t, c):
+        at = ja + t
+        src = slabs.at[c] if t == 0 else row_slabs.at[at, c]
+        return remote(src, row_slabs.at[at, c], dn_s.at[t, c], dn_r.at[t, c], (ia, ja - 1))
+
+    def send_rows(t, c, act):
+        @pl.when((ja + 1 < n_ja) & (ja - t >= 0))
+        def _():
+            act(up(t, c))
+
+        @pl.when((ja >= 1) & (ja + t < n_ja))
+        def _():
+            act(down(t, c))
+
+    def take_rows(t, c):
+        @pl.when(ja - 1 - t >= 0)
+        def _():
+            pltpu.make_async_copy(
+                slabs.at[c], row_slabs.at[ja - 1 - t, c], up_r.at[t, c]
+            ).wait()
+
+        @pl.when(ja + 1 + t < n_ja)
+        def _():
+            pltpu.make_async_copy(
+                slabs.at[c], row_slabs.at[ja + 1 + t, c], dn_r.at[t, c]
+            ).wait()
+
     cols = [
         remote(slabs, col_slabs.at[ia], col_s.at[k], col_r.at[k],
                (lax.rem(ia + 2 * k, n_ia), ja))
@@ -75,8 +105,14 @@
         remote(ask_j.at[0], all_j.at[ja], aj_s.at[k], aj_r.at[k], (ia, lax.rem(ja + k, n_ja)))
         for k in range(1, n_ja)
     ]
-    for c in cols + rows + [own] + asks:
-        c.start()
+    for c in range(blocks):
+        send_rows(0, c, lambda copy: copy.start())
+    for c in cols + [own] + asks:
+        c.start()
+    for t in range(n_ja - 2):
+        for c in range(blocks):
+            take_rows(t, c)
+            send_rows(t + 1, c, lambda copy: copy.start())
     forwards = [own]
     for k in range(1, half):
         source = lax.rem(ia + n_ia - 2 * k, n_ia)
@@ -87,27 +123,32 @@
         forwards.append(f)
     for c in locals_:
         c.wait()
-    for c in rows + forwards:
+    for c in forwards:
         c.wait_recv()
 
-    def project(p, carry):
-        f, s, d0, d1 = first[p], second[p], dom[p, 0], dom[p, 1]
-        both = jnp.concatenate(
-            [
-                jnp.concatenate([row_slabs[f, d0], row_slabs[f, d1]], axis=0),
-                jnp.concatenate([col_slabs[s, d0], col_slabs[s, d1]], axis=0),
-            ],
-            axis=1,
-        )
-        projected = matmul(coef[p], both, 0, 0).astype(BF16)
-        aux = projected.shape[1] // 2
-        exch[p] = matmul(projected[:, :aux], projected[:, aux:], 1, 1)
+    def gathered(table, o, p):
+        return jnp.concatenate([table[o, dom[0, p]], table[o, dom[1, p]]], axis=0)
+
+    def project_second(p, carry):
+        proj[p] = matmul(coef[p], gathered(col_slabs, second[p], p), 0, 0).astype(BF16)
         return carry
 
-    lax.fori_loop(0, coef.shape[0], project, 0)
+    lax.fori_loop(0, coef.shape[0], project_second, 0)
+    for c in range(blocks):
+        take_rows(n_ja - 2, c)
+
+    def project_first(p, carry):
+        projected = matmul(coef[p], gathered(row_slabs, first[p], p), 0, 0).astype(BF16)
+        exch[p] = matmul(projected, proj[p], 1, 1)
+        return carry
+
+    lax.fori_loop(0, coef.shape[0], project_first, 0)
     for c in asks:
         c.wait_recv()
-    for c in rows + cols + forwards + asks:
+    for t in range(n_ja - 1):
+        for c in range(blocks):
+            send_rows(t, c, lambda copy: copy.wait_send())
+    for c in cols + forwards + asks:
         c.wait_send()
 
 
@@ -121,7 +162,7 @@
 ):
     ia, ja = lax.axis_index("ia"), lax.axis_index("ja")
     pairs = exch.shape[0]
-    slots_i, slots_j = all_i.shape[2], all_j.shape[2]
+    slots_i, slots_j = all_i.shape[1], all_j.shape[2]
     loads = [
         pltpu.make_async_copy(margin_j, mj, m_sem.at[0]),
         pltpu.make_async_copy(margin_i, mi, m_sem.at[1]),
@@ -168,7 +209,7 @@
         for k in range(1, n_ia):
             peer = lax.rem(ia + k, n_ia)
             for slot in range(slots_i):
-                stage_i[it, k, slot] = sent[all_i[peer, ia, slot]]
+                stage_i[it, k, slot] = sent[all_i[peer, slot, ia]]
             c = remote(stage_i.at[it, k], table_i.at[pl.ds(ia * slots_i, slots_i)],
                        is_.at[it, k], ir_.at[it, k], (peer, ja))
             c.start()
@@ -176,7 +217,7 @@
         for slot in range(slots_j):
             table_j[ja * slots_j + slot] = sent[all_j[ja, ja, slot]]
         for slot in range(slots_i):
-            table_i[ia * slots_i + slot] = sent[all_i[ia, ia, slot]]
+            table_i[ia * slots_i + slot] = sent[all_i[ia, slot, ia]]
         if it == 0:
             loads[0].wait()
         for c in copies_j:
@@ -211,7 +252,7 @@
         square = (matmul(s, s, 1, 1) + matmul(s, s, 0, 0)).astype(BF16)
         c = coef[p]
         mapped = matmul(c, square, 1, 0).astype(BF16)
-        d0, d1 = dom[p, 0], dom[p, 1]
+        d0, d1 = dom[0, p], dom[1, p]
         for b in range(blocks):
             k0 = jnp.where(d0 == b, 1.0, 0.0).astype(F32)
             k1 = jnp.where(d1 == b, 1.0, 0.0).astype(F32)
@@ -275,6 +316,8 @@
     blocks = pao // BLK
     slots_i, slots_j = ask_i.shape[2], ask_j.shape[2]
     links_i, links_j = margin_i.shape[1], margin_j.shape[1]
+    ask_i = ask_i.transpose(0, 2, 1)
+    dom_blocks = dom_blocks.T
     vmem = pl.BlockSpec(memory_space=pltpu.VMEM)
     smem = pl.BlockSpec(memory_space=pltpu.SMEM)
     anym = pl.BlockSpec(memory_space=pl.ANY)
@@ -292,8 +335,10 @@
         scratch_shapes=[
             pltpu.VMEM((n_ja, blocks, BLK, aux), BF16),
             pltpu.VMEM((n_ia, blocks, BLK, aux), BF16),
+            pltpu.VMEM((pairs, pno, aux), BF16),
             dma((4,)),
-            dma((n_ja,)), dma((n_ja,)),
+            dma((n_ja, blocks)), dma((n_ja, blocks)),
+            dma((n_ja, blocks)), dma((n_ja, blocks)),
             dma((n_ia,)), dma((n_ia,)),
             dma((n_ia,)), dma((n_ia,)),
             dma((n_ia,)), dma((n_ia,)),

time: 158 us -> 142 us (0.90)
  Pallas kernels: 151 us -> 137 us
  local copies, waits for them, and re-layouts: 6.37 us -> 3.67 us
    pallas_call x1, Pallas kernels: 94.5 us -> 87.7 us  [body(): pl.pallas_call(functools.partial(amplitude_kernel, n_ia, n_ja, factor), o...]
    pallas_call x1, Pallas kernels: 56 us -> 49.7 us  [body(): pl.pallas_call(functools.partial(exchange_kernel, n_ia, n_ja), out_shape=...]
    unnamed x4 -> x2, local copies, waits for them, and re-layouts: 6.37 us -> 3.67 us
where the time goes in v1:
time: 142 us
  Pallas kernels  137 us (96%)
  local copies, waits for them, and re-layouts  3.67 us (3%)
    pallas_call x1, Pallas kernels, body(): pl.pallas_call(functools.partial(amplitude_kernel, n_ia, n_ja, factor), o...  87.7 us
    pallas_call x1, Pallas kernels, body(): pl.pallas_call(functools.partial(exchange_kernel, n_ia, n_ja), out_shape=...  49.7 us
    unnamed x2, local copies, waits for them, and re-layouts  3.67 us

profile of v1, /device:TPU:0, one launch (start us, length us, event | category | flops | bytes accessed | tf_op | source)
XLA Modules:
  0.0 141.7 jit_solution(1219801463072367293)
XLA Ops:
  0.6 49.7 %exchange.1 = (f32[16,128,128]{2,1,0:T(8,128)}, s32[8,4,8]{2,1,0:T(4,128)}, s32[4,4,4]{2,1,0:T(4,128)}) custom-call(bf16[4,128,512]{2,1,0:T(8,128)(2,1)} %bitcast.3, s32[1,4,8]{2,1,0:T(4,128)} %bitcast.6, s32[1,4,4]{2,1,0:T(4,128)} %ask_j.1, bf16[16,256,128]{2,1,0:T(8,128)(2,1)} %coef.3, s32[2,16]{1,0:T(2,128)} %bitcast.4, s32[16]{0:T(128)} %first.1, s32[16]{0:T(128)} %second.1), custom_call_target="tpu_custom_call" | custom-call | tf_op jit(solution)/shard_map/exchange/pallas_call | solution.py:326
  50.3 87.7 %amplitudes.1 = (f32[16,128,128]{2,1,0:T(8,128)}, f32[16,512]{1,0:T(8,128)}) custom-call(f32[16,128,128]{2,1,0:T(8,128)} %get-tuple-element.5.exch, f32[16,128]{1,0:T(8,128)} %energy.1, f32[16]{0:T(128)} %shift.1, bf16[16,256,128]{2,1,0:T(8,128)(2,1)} %coef.3, bf16[16,16,128,128]{3,2,1,0:T(8,128)(2,1)} %margin_i.1, bf16[16,16,128,128]{3,2,1,0:T(8,128)(2,1)} %margin_j.1, ...), custom_call_target="tpu_custom_call" | custom-call | tf_op jit(solution)/shard_map/amplitudes/pallas_call | solution.py:353
  138.0 2.3 %copy.19 = f32[16,128,128]{2,1,0:T(8,128)} copy(f32[16,128,128]{2,1,0:T(8,128)} %get-tuple-element.10) | data formatting | bytes 2097152
  140.3 1.4 copy.20

commit v2 on v1

--- a/solution.py
+++ b/solution.py
@@ -142,7 +142,7 @@
         exch[p] = matmul(projected, proj[p], 1, 1)
         return carry
 
-    lax.fori_loop(0, coef.shape[0], project_first, 0)
+    lax.fori_loop(0, coef.shape[0], project_first, 0, unroll=4)
     for c in asks:
         c.wait_recv()
     for t in range(n_ja - 1):
@@ -227,7 +227,7 @@
             acc[p] = couple(p, table_j, mj, cpl_j, link_j, None)
             return carry
 
-        lax.fori_loop(0, pairs, second_kind, 0)
+        lax.fori_loop(0, pairs, second_kind, 0, unroll=4)
         if it == 0:
             loads[1].wait()
         for c in copies_i:
@@ -241,7 +241,7 @@
             sent[p] = new.astype(BF16)
             return carry
 
-        lax.fori_loop(0, pairs, first_kind, 0)
+        lax.fori_loop(0, pairs, first_kind, 0, unroll=4)
         for c in copies_i + copies_j:
             c.wait_send()
 
@@ -263,7 +263,7 @@
             cf[p, where] = (c[:BLK].astype(F32) * k0 + c[BLK:].astype(F32) * k1).astype(BF16)
         return carry
 
-    lax.fori_loop(0, pairs, spread, 0)
+    lax.fori_loop(0, pairs, spread, 0, unroll=4)
     chunk = own.shape[0]
 
     def partial_rows(peer):
@@ -289,17 +289,17 @@
         own[...] += in1[k].astype(F32)
     piece = dens.shape[0]
     for j in range(n_ja):
-        out2[j] = own[pl.ds(j * piece, piece), :]
+        out2[j] = own[pl.ds(j * piece, piece), :].astype(BF16)
     last = []
     for k in range(1, n_ja):
         peer = lax.rem(ja + k, n_ja)
         c = remote(out2.at[peer], in2.at[k], s2.at[k], r2.at[k], (ia, peer))
         c.start()
         last.append(c)
-    total = out2[ja]
+    total = out2[ja].astype(F32)
     for k in range(1, n_ja):
         last[k - 1].wait_recv()
-        total = total + in2[k]
+        total = total + in2[k].astype(F32)
     dens[...] = total * factor
     for c in sends + last:
         c.wait_send()
@@ -372,8 +372,8 @@
             pltpu.VMEM((chunk, pao), F32),
             pltpu.VMEM((n_ia, chunk, pao), BF16),
             pltpu.VMEM((n_ia, chunk, pao), BF16),
-            pltpu.VMEM((n_ja, piece, pao), F32),
-            pltpu.VMEM((n_ja, piece, pao), F32),
+            pltpu.VMEM((n_ja, piece, pao), BF16),
+            pltpu.VMEM((n_ja, piece, pao), BF16),
             dma((2,)),
             dma((ITERS, n_ia)), dma((ITERS, n_ia)),
             dma((ITERS, n_ja)), dma((ITERS, n_ja)),

time: 142 us -> 120 us (0.85)
  Pallas kernels: 137 us -> 116 us
    pallas_call x1, Pallas kernels: 87.7 us -> 69.3 us  [body(): pl.pallas_call(functools.partial(amplitude_kernel, n_ia, n_ja, factor), o...]
    pallas_call x1, Pallas kernels: 49.7 us -> 46.2 us  [body(): pl.pallas_call(functools.partial(exchange_kernel, n_ia, n_ja), out_shape=...]
where the time goes in v2:
time: 120 us
  Pallas kernels  116 us (97%)
  local copies, waits for them, and re-layouts  3.67 us (3%)
    pallas_call x1, Pallas kernels, body(): pl.pallas_call(functools.partial(amplitude_kernel, n_ia, n_ja, factor), o...  69.3 us
    pallas_call x1, Pallas kernels, body(): pl.pallas_call(functools.partial(exchange_kernel, n_ia, n_ja), out_shape=...  46.2 us
    unnamed x2, local copies, waits for them, and re-layouts  3.67 us

profile of v2, /device:TPU:0, one launch (start us, length us, event | category | flops | bytes accessed | tf_op | source)
XLA Modules:
  0.0 119.9 jit_solution(8623695025197037629)
XLA Ops:
  0.6 46.2 %exchange.1 = (f32[16,128,128]{2,1,0:T(8,128)}, s32[8,4,8]{2,1,0:T(4,128)}, s32[4,4,4]{2,1,0:T(4,128)}) custom-call(bf16[4,128,512]{2,1,0:T(8,128)(2,1)} %bitcast.3, s32[1,4,8]{2,1,0:T(4,128)} %bitcast.6, s32[1,4,4]{2,1,0:T(4,128)} %ask_j.1, bf16[16,256,128]{2,1,0:T(8,128)(2,1)} %coef.3, s32[2,16]{1,0:T(2,128)} %bitcast.4, s32[16]{0:T(128)} %first.1, s32[16]{0:T(128)} %second.1), custom_call_target="tpu_custom_call" | custom-call | tf_op jit(solution)/shard_map/exchange/pallas_call | solution.py:326
  46.9 69.3 %amplitudes.1 = (f32[16,128,128]{2,1,0:T(8,128)}, f32[16,512]{1,0:T(8,128)}) custom-call(f32[16,128,128]{2,1,0:T(8,128)} %get-tuple-element.5.exch, f32[16,128]{1,0:T(8,128)} %energy.1, f32[16]{0:T(128)} %shift.1, bf16[16,256,128]{2,1,0:T(8,128)(2,1)} %coef.3, bf16[16,16,128,128]{3,2,1,0:T(8,128)(2,1)} %margin_i.1, bf16[16,16,128,128]{3,2,1,0:T(8,128)(2,1)} %margin_j.1, ...), custom_call_target="tpu_custom_call" | custom-call | tf_op jit(solution)/shard_map/amplitudes/pallas_call | solution.py:353
  116.2 2.3 %copy.19 = f32[16,128,128]{2,1,0:T(8,128)} copy(f32[16,128,128]{2,1,0:T(8,128)} %get-tuple-element.10) | data formatting | bytes 2097152
  118.5 1.4 %copy.20 = f32[16,512]{1,0:T(8,128)} copy(f32[16,512]{1,0:T(8,128)} %get-tuple-element.11) | data formatting | bytes 65536
